TPU v7x, 32 devices: a whole 2x2x4 slice. The times are simulated.
32 devices in a mesh: grp: 2 (over y), node: 4 (over z), rank: 4 (over x, core).
Axes of the slice: x: 2, y: 2, z: 4, core: 2. Of those that a mesh axis runs over, the one named last changes fastest.
Arguments:
- tokens: bfloat16 [1024, 2048], P(('grp', 'node', 'rank')), parts along dimension 0, may hold values from -6 to 6
- expert_ids: int32 [1024, 10], P(('grp', 'node', 'rank')), parts along dimension 0, may hold values from 0 to 31, all different within a row; in each aligned block of 32 rows (0 to 31, 32 to 63, ...) at most 15 rows name the same one
- combine_weights: int32 [1024, 10], P(('grp', 'node', 'rank')), parts along dimension 0, may hold values from 16384 to 65535
- slot_plan: int32 [32], replicated, may hold values from 0 to 31, each once
- w_gate: bfloat16 [32, 2048, 512], P(('node', 'rank')), may hold values from -0.125 to 0.125
- w_up: bfloat16 [32, 2048, 512], P(('node', 'rank')), may hold values from -0.125 to 0.125
- w_down: bfloat16 [32, 512, 2048], P(('node', 'rank')), may hold values from -0.25 to 0.25
Outputs:
- mixed: bfloat16 [1024, 2048], P(('grp', 'node', 'rank')), parts along dimension 0
There are 2 independent parts, one for each index of `grp`. A program takes and returns all parts, laid end to end along the dimension named above; an argument that names none is the same for every part. Nothing has to cross between parts.
Inputs may be any that keep to these rules, and one draw needn't show every extreme that they name: `expert_ids`: each row names 10 different experts; among the rows of one device no expert is named more than 15 times, and in every draw some expert reaches 15. `slot_plan`: each slot once.
All inputs are finite; a program needn't handle non-finite values.
Results may differ from a plain program's by a relative error of at most 0.0058.
Values may be sent and summed in bfloat16 or wider, within the bound.
A program may use at most 64 MiB of HBM per device.

v0:
```python
import jax
import jax.numpy as jnp
from jax import lax
from jax.sharding import PartitionSpec as P


def local(tokens, expert_ids, combine_weights, slot_plan, w_gate, w_up, w_down):
    n_node = lax.axis_size("node")
    n_rank = lax.axis_size("rank")
    n_dev = n_node * n_rank
    exp_dev = w_gate.shape[0]
    slots = n_dev * exp_dev
    tok_rows, top = expert_ids.shape
    width = tokens.shape[1]
    capacity = max(2, (3 * tok_rows * top + 2 * slots - 1) // (2 * slots))
    flat_ids = expert_ids.reshape(-1)
    onehot = (flat_ids[:, None] == jnp.arange(slots, dtype=jnp.int32)[None, :]).astype(jnp.int32)
    slot_of = jnp.sum(onehot * slot_plan[None, :], axis=1)
    earlier = jnp.cumsum(onehot, axis=0) - onehot
    position = jnp.sum(earlier * onehot, axis=1)
    target = slot_of * capacity + position
    repeated = jnp.repeat(tokens, top, axis=0)
    outgoing = jnp.zeros((slots * capacity, width), jnp.bfloat16).at[target].set(repeated)
    flat_out = outgoing.reshape(n_dev, exp_dev * capacity, width)
    arrived = lax.all_to_all(flat_out, ("node", "rank"), split_axis=0, concat_axis=0, tiled=True)
    arrived = arrived.reshape(n_dev, exp_dev, capacity, width)
    gate = jnp.einsum("secd,edf->secf", arrived, w_gate, preferred_element_type=jnp.float32)
    up = jnp.einsum("secd,edf->secf", arrived, w_up, preferred_element_type=jnp.float32)
    hidden = (jax.nn.silu(gate) * up).astype(jnp.bfloat16)
    result = jnp.einsum(
        "secf,efd->secd", hidden, w_down, preferred_element_type=jnp.float32
    ).astype(jnp.bfloat16)
    flat_back = result.reshape(n_dev, exp_dev * capacity, width)
    returned = lax.all_to_all(flat_back, ("node", "rank"), split_axis=0, concat_axis=0, tiled=True)
    returned = returned.reshape(slots * capacity, width)
    picked = returned[target].reshape(tok_rows, top, width)
    scales = combine_weights.astype(jnp.float32) / 65536.0
    mixed = jnp.sum(picked.astype(jnp.float32) * scales[:, :, None], axis=1)
    return mixed.astype(jnp.bfloat16)


def solution(mesh):
    in_specs = (
        P(("grp", "node", "rank"), None),
        P(("grp", "node", "rank"), None),
        P(("grp", "node", "rank"), None),
        P(),
        P(("node", "rank"), None, None),
        P(("node", "rank"), None, None),
        P(("node", "rank"), None, None),
    )
    out_specs = P(("grp", "node", "rank"), None)
    return jax.shard_map(local, mesh=mesh, in_specs=in_specs, out_specs=out_specs, check_vma=False)
```

profile of v0, /device:TPU:11, one launch (start us, length us, event | category | flops | bytes accessed | tf_op | source)
XLA Modules:
  0.0 140.9 jit_solution(4044873898874885216)
XLA Ops:
  0.0 0.8 copy.10
  0.8 0.1 eq.22
  0.9 0.9 reduce-window.6
  1.8 0.2 slice_reduce_fusion
  2.1 0.1 bitcast_bitcast_fusion
  2.1 0.8 select_reduce_fusion
  2.9 1.2 broadcast_in_dim.5
  4.1 0.5 reshape.79
  4.6 4.0 %scatter_custom_fusion = bf16[480,2048]{1,0:T(8,128)(2,1)} fusion(s32[320]{0:T(512)S(1)} %fusion.28, bf16[320,2048]{1,0:T(8,128)(2,1)S(1)} %reshape.79, bf16[]{:T(256)} %constant.7.clone.1), kind=kCustom, calls=%fused_computation.14 | custom fusion | bytes 1966082 | tf_op jit(solution)/shard_map/scatter | solution.py:23
  8.6 1.8 %reshape.61 = bf16[16,30,2048]{2,1,0:T(8,128)(2,1)S(1)} reshape(bf16[480,2048]{1,0:T(8,128)(2,1)} %scatter_custom_fusion) | data formatting | bytes 3932160 | tf_op jit(solution)/shard_map/reshape | solution.py:24
  10.4 0.0 copy-start.1
  10.4 53.9 %all_to_all.10 = bf16[16,30,2048]{2,1,0:T(8,128)(2,1)S(1)} all-to-all(bf16[16,30,2048]{2,1,0:T(8,128)(2,1)S(1)} %reshape.61), channel_id=1, replica_groups=mesh['grp'=2,'node'=4,'rank'=4] {'node','rank'}, dimensions={0} | all-to-all | bytes 3932160 | tf_op jit(solution)/shard_map/all_to_all | solution.py:25
  64.2 1.1 copy.13
  65.3 0.0 copy-done.1
  65.3 1.2 fusion.9
  66.6 7.1 %fusion.6 = bf16[2,16,15,2048]{3,1,2,0:T(8,128)(2,1)} fusion(bf16[2,512,2048]{2,1,0:T(8,128)(2,1)} %param.13, bf16[16,2,15,2048]{3,0,2,1:T(8,128)(2,1)S(1)} %bitcast.57, bf16[2,2048,512]{2,1,0:T(8,128)(2,1)} %param.12, f32[16,2,15,512]{3,0,2,1:T(8,128)S(1)} %fusion.9), kind=kOutput, calls=%fused_computation.9 | convolution fusion | flops 2015723520 | bytes 13303808 | tf_op jit(solution)/shard_map/secf,efd->secd/dot_general | solution.py:30
  73.7 4.0 %copy.14 = bf16[16,30,2048]{2,1,0:T(8,128)(2,1)} copy(bf16[16,30,2048]{2,0,1:T(8,128)(2,1)} %bitcast.58) | data formatting | bytes 3932160 | tf_op jit(solution)/shard_map/reshape | solution.py:33
  77.6 0.0 copy-start
  77.6 5.2 %all-to-all-start.1 = ((bf16[16,30,2048]{2,1,0:T(8,128)(2,1)}), bf16[16,30,2048]{2,1,0:T(8,128)(2,1)}, u32[]{:S(2)}, u32[]{:S(2)}) async-start(bf16[16,30,2048]{2,1,0:T(8,128)(2,1)} %copy.14), calls=%async_computation.1 | async-start | bytes 4194304 | tf_op jit(solution)/shard_map/all_to_all | solution.py:34
  82.8 0.0 copy-done
  82.8 0.1 copy.15
  82.9 47.4 %all-to-all-done.1 = bf16[16,30,2048]{2,1,0:T(8,128)(2,1)} async-done(((bf16[16,30,2048]{2,1,0:T(8,128)(2,1)}), bf16[16,30,2048]{2,1,0:T(8,128)(2,1)}, u32[]{:S(2)}, u32[]{:S(2)}) %all-to-all-start.1) | async-done | bytes 1966112 | tf_op jit(solution)/shard_map/all_to_all | solution.py:34
  130.3 1.8 %reshape.64 = bf16[480,2048]{1,0:T(8,128)(2,1)S(1)} reshape(bf16[16,30,2048]{2,1,0:T(8,128)(2,1)} %all-to-all-done.1) | data formatting | bytes 3932160 | tf_op jit(solution)/shard_map/reshape | solution.py:35
  132.1 2.4 %gather_fusion = bf16[320,2048]{1,0:T(8,128)(2,1)S(1)} fusion(bf16[480,2048]{1,0:T(8,128)(2,1)S(1)} %reshape.64, s32[1024]{0:T(1024)S(1)} %pad_clamp_fusion), kind=kCustom, calls=%fused_computation | custom fusion | bytes 2622720 | tf_op jit(solution)/shard_map/gather | solution.py:36
  134.6 2.1 %reshape.66 = f32[32,10,2048]{2,1,0:T(8,128)} reshape(bf16[320,2048]{1,0:T(8,128)(2,1)S(1)} %gather_fusion) | data formatting | bytes 3932160 | tf_op jit(solution)/shard_map/convert_element_type | solution.py:38
  136.7 4.3 %multiply_reduce_fusion = bf16[32,2048]{1,0:T(8,128)(2,1)} fusion(f32[32,10,2048]{2,1,0:T(8,128)} %reshape.66, f32[32,10]{1,0:T(8,128)S(1)} %copy.15), kind=kLoop, calls=%fused_computation.8 | loop fusion | flops 1245184 | bytes 2753792 | tf_op jit(solution)/shard_map/reduce_sum | solution.py:38
  (7 shorter events, 0.1 us)
Async XLA Ops:
  10.4 55.0 %copy-start.1 = (bf16[2,2048,512]{2,1,0:T(8,128)(2,1)S(1)}, bf16[2,2048,512]{2,1,0:T(8,128)(2,1)}, u32[]{:S(2)}) copy-start(bf16[2,2048,512]{2,1,0:T(8,128)(2,1)} %param.11) | copy-start | bytes 12582916
  77.6 5.2 %copy-start = (s32[32,10]{0,1:T(8,128)S(1)}, s32[32,10]{0,1:T(8,128)}, u32[]{:S(2)}) copy-start(s32[32,10]{0,1:T(8,128)} %param.9) | copy-start | bytes 3844
  77.6 52.7 %all-to-all-start.1 = ((bf16[16,30,2048]{2,1,0:T(8,128)(2,1)}), bf16[16,30,2048]{2,1,0:T(8,128)(2,1)}, u32[]{:S(2)}, u32[]{:S(2)}) async-start(bf16[16,30,2048]{2,1,0:T(8,128)(2,1)} %copy.14), calls=%async_computation.1 | async-start | bytes 4194304 | tf_op jit(solution)/shard_map/all_to_all | solution.py:34
where the time goes:
time: 141 us
  blocking collectives  53.9 us (38%)
  waiting for transfers between devices  47.4 us (34%)
  local copies, waits for them, and re-layouts  20 us (14%)
  matrix products  8.31 us (6%)
  other arithmetic  6.06 us (4%)
  starting transfers between devices  5.16 us (4%)
    all_to_all x1, blocking collectives, local(): lax.all_to_all(flat_out, ('node', 'rank'), split_axis=0, concat_axis=0, t...  53.9 us
    all_to_all x1, waiting for transfers between devices, local(): lax.all_to_all(flat_back, ('node', 'rank'), split_axis=0, concat_axis=0,...  47.4 us
    dot_general x1, matrix products, local(): jnp.einsum('secf,efd->secd', hidden, w_down, preferred_element_type=jnp.f...  7.09 us
    all_to_all x1, starting transfers between devices, local(): lax.all_to_all(flat_back, ('node', 'rank'), split_axis=0, concat_axis=0,...  5.16 us
    reduce_sum x1, other arithmetic, local(): mixed = jnp.sum(picked.astype(jnp.float32) * scales[:, :, None], axis=1)  4.25 us
    scatter x1, local copies, waits for them, and re-layouts, local(): jnp.zeros((slots * capacity, width), jnp.bfloat16).at[target].set(repeated)  4 us
    reshape x1, local copies, waits for them, and re-layouts, local(): flat_back = result.reshape(n_dev, exp_dev * capacity, width)  3.98 us
  transfers between devices with their start and end apart: 1, of which 1 were waited for; matrix products, arithmetic and copies ran while one was open for 0% of the time, Pallas kernels for 0%

commit v1 on v0

--- a/solution.py
+++ b/solution.py
@@ -1,10 +1,18 @@
+import functools
 import jax
 import jax.numpy as jnp
 from jax import lax
+from jax.experimental import pallas as pl
+from jax.experimental.pallas import tpu as pltpu
 from jax.sharding import PartitionSpec as P
 
-
-def local(tokens, expert_ids, combine_weights, slot_plan, w_gate, w_up, w_down):
+CORES = 2
+CHUNKS = 4
+MESH = pl.DeviceIdType.MESH
+UP, DOWN, CROSS, TWIN, RELAY = range(5)
+
+
+def sparse_local(tokens, expert_ids, combine_weights, slot_plan, w_gate, w_up, w_down):
     n_node = lax.axis_size("node")
     n_rank = lax.axis_size("rank")
     n_dev = n_node * n_rank
@@ -39,6 +47,342 @@
     return mixed.astype(jnp.bfloat16)
 
 
+def kernel(
+    nz, experts, tok_hbm, ids_ref, wts_ref, plan_ref, wg_hbm, wu_hbm, wd_hbm, out_ref,
+    *scratch,
+):
+    bufs = scratch[:CHUNKS]
+    (wgu, wdn, acc, hid, s1, r1, k1, s2, r2, az, su, ru, sd, rd,
+     own_sem, wgu_sem, wd_sem, send_sem, recv_sem,
+     s1_sem, r1_sem, s2_sem, r2_sem, su_sem, ru_sem, sd_sem, rd_sem) = scratch[CHUNKS:]
+    z = lax.axis_index("node")
+    rank = lax.axis_index("rank")
+    x, c = rank // CORES, rank % CORES
+    rows, width = tok_hbm.shape
+    cols = width // CHUNKS
+    exp_dev, _, ff = wg_hbm.shape
+    col_rows = nz * rows
+    half = 2 * nz
+    total_rows = 2 * half * rows
+    mine = c * half + x * nz
+    other = c * half + (1 - x) * nz
+    above, below = {"node": z + 1}, {"node": z - 1}
+    across = {"rank": (1 - x) * CORES + c}
+    twin = {"rank": x * CORES + (1 - c)}
+
+    own = [
+        pltpu.make_async_copy(
+            tok_hbm.at[:, pl.ds(j * cols, cols)],
+            bufs[j].at[mine + z, :, pl.ds(0, cols)],
+            own_sem.at[j],
+        )
+        for j in range(CHUNKS)
+    ]
+    for copy in own:
+        copy.start()
+
+    barrier = pltpu.get_barrier_semaphore()
+
+    def greet(device):
+        pl.semaphore_signal(barrier, inc=1, device_id=device, device_id_type=MESH)
+
+    greet(across)
+    greet(twin)
+    pl.when(z < nz - 1)(lambda: greet(above))
+    pl.when(z > 0)(lambda: greet(below))
+
+    gu_copies = []
+    for j in range(CHUNKS):
+        piece = []
+        for e in range(exp_dev):
+            for g, src in enumerate((wg_hbm, wu_hbm)):
+                i = e * 2 + g
+                piece.append(pltpu.make_async_copy(
+                    src.at[e, pl.ds(j * cols, cols), :],
+                    wgu.at[i, pl.ds(j * cols, cols), :],
+                    wgu_sem.at[j, i],
+                ))
+        gu_copies.append(piece)
+    d_copies = [
+        pltpu.make_async_copy(wd_hbm.at[e], wdn.at[pl.ds(e * ff, ff), :], wd_sem.at[e])
+        for e in range(exp_dev)
+    ]
+    for piece in gu_copies:
+        for copy in piece:
+            copy.start()
+    for copy in d_copies:
+        copy.start()
+
+    mix_w = bufs[0].shape[2] - cols
+    lane = lax.broadcasted_iota(jnp.int32, (rows, mix_w), 1)
+    low = lane >= experts
+    expert = jnp.where(low, lane - experts, lane)
+    ids, wts = ids_ref[...], wts_ref[...]
+    dense = jnp.zeros((rows, mix_w), jnp.int32)
+    for k in range(ids.shape[1]):
+        dense += jnp.where(ids[:, k:k + 1] == expert, wts[:, k:k + 1], 0)
+    parts = jnp.where(low, dense & 255, dense >> 8)
+    bufs[0][mine + z, :, cols:] = parts.astype(jnp.float32).astype(jnp.bfloat16)
+
+    peers = 2 + (z < nz - 1).astype(jnp.int32) + (z > 0).astype(jnp.int32)
+    pl.semaphore_wait(barrier, peers)
+
+    def block_copy(j, slot, kind, row, device):
+        return pltpu.make_async_remote_copy(
+            src_ref=bufs[j].at[slot],
+            dst_ref=bufs[j].at[slot],
+            send_sem=send_sem.at[j, kind, row],
+            recv_sem=recv_sem.at[j, slot],
+            device_id=device,
+            device_id_type=MESH,
+        )
+
+    def arrived(j, slot):
+        block_copy(j, slot, RELAY, 0, twin).wait_recv()
+
+    def spread(j, src, go_up, go_down):
+        if go_up:
+            pl.when(z < nz - 1)(lambda: block_copy(j, mine + src, UP, src, above).start())
+        if go_down:
+            pl.when(z > 0)(lambda: block_copy(j, mine + src, DOWN, src, below).start())
+        block_copy(j, mine + src, CROSS, src, across).start()
+        block_copy(j, mine + src, TWIN, src, twin).start()
+
+    def relay(j, src):
+        arrived(j, other + src)
+        block_copy(j, other + src, RELAY, src, twin).start()
+
+    def gather_step(j, dist):
+        if dist == 0:
+            own[j].wait()
+            spread(j, z, True, True)
+        elif dist < nz:
+            @pl.when(z - dist >= 0)
+            def _():
+                arrived(j, mine + z - dist)
+                spread(j, z - dist, True, False)
+
+            @pl.when(z + dist <= nz - 1)
+            def _():
+                arrived(j, mine + z + dist)
+                spread(j, z + dist, False, True)
+        if dist >= 1:
+            if dist == 1:
+                relay(j, z)
+            else:
+                pl.when(z - dist + 1 >= 0)(lambda: relay(j, z - dist + 1))
+                pl.when(z + dist - 1 <= nz - 1)(lambda: relay(j, z + dist - 1))
+
+    def project(j):
+        for s in range(half):
+            arrived(j, (1 - c) * half + s)
+        for copy in gu_copies[j]:
+            copy.wait()
+
+        def one(i, carry):
+            block = bufs[j][:, :, :cols].reshape(total_rows, cols)
+            part = jnp.dot(
+                block, wgu[i, pl.ds(j * cols, cols), :], preferred_element_type=jnp.float32
+            )
+            if j == 0:
+                acc[i] = part
+            else:
+                acc[i] = acc[i] + part
+            return carry
+
+        lax.fori_loop(0, 2 * exp_dev, one, 0)
+
+    for wave in range(CHUNKS + nz):
+        for dist in range(nz + 1):
+            j = wave - dist
+            if 0 <= j < CHUNKS:
+                gather_step(j, dist)
+        if 0 <= wave - nz < CHUNKS:
+            project(wave - nz)
+
+    device = z * lax.axis_size("rank") + rank
+    mixes = bufs[0][:, :, cols:].reshape(total_rows, mix_w).astype(jnp.float32)
+    lane_row = lax.broadcasted_iota(jnp.int32, (1, mix_w), 1)
+    unit = jnp.where(lane_row < experts, 256.0 / 65536.0, 1.0 / 65536.0)
+    for e in range(exp_dev):
+        pick = jnp.where(plan_ref[...] == device * exp_dev + e, unit, 0.0)
+        scale = jnp.sum(mixes * pick, axis=1, keepdims=True)
+        gate = acc[2 * e]
+        value = gate / (1.0 + jnp.exp(-gate)) * acc[2 * e + 1]
+        hid[:, e * ff:(e + 1) * ff] = (value * scale).astype(jnp.bfloat16)
+    for copy in d_copies:
+        copy.wait()
+
+    half_rows = half * rows
+
+    def push(src, dst, ssem, rsem, dev):
+        return pltpu.make_async_remote_copy(
+            src_ref=src, dst_ref=dst, send_sem=ssem, recv_sem=rsem,
+            device_id=dev, device_id_type=MESH,
+        )
+
+    def twin_copy(j):
+        return push(s1.at[j], r1.at[j], s1_sem.at[j], r1_sem.at[j], twin)
+
+    def cross_copy(j):
+        return push(s2.at[j], r2.at[j], s2_sem.at[j], r2_sem.at[j], across)
+
+    def up_copy(j, t):
+        return push(su.at[j, t], ru.at[j, t], su_sem.at[j, t], ru_sem.at[j, t], above)
+
+    def down_copy(j, t):
+        return push(sd.at[j, t], rd.at[j, t], sd_sem.at[j, t], rd_sem.at[j, t], below)
+
+    def stage_down(j):
+        w = wdn[:, j * cols:(j + 1) * cols]
+        s1[j] = jnp.dot(
+            hid[pl.ds((1 - c) * half_rows, half_rows), :], w, preferred_element_type=jnp.float32
+        ).astype(jnp.bfloat16)
+        twin_copy(j).start()
+        k1[j] = jnp.dot(
+            hid[pl.ds(c * half_rows, half_rows), :], w, preferred_element_type=jnp.float32
+        )
+
+    def stage_cross(j):
+        twin_copy(j).wait_recv()
+        away = pl.ds((1 - x) * col_rows, col_rows)
+        s2[j] = (k1[j, away, :] + r1[j, away, :].astype(jnp.float32)).astype(jnp.bfloat16)
+        cross_copy(j).start()
+
+    def stage_column(j):
+        cross_copy(j).wait_recv()
+        near = pl.ds(x * col_rows, col_rows)
+        total = k1[j, near, :] + r1[j, near, :].astype(jnp.float32) + r2[j].astype(jnp.float32)
+        az[j] = total.reshape(nz, rows, cols)
+
+    def stage_chain(j):
+        for t in range(nz - 1, 0, -1):
+            @pl.when(z == 0)
+            def _():
+                su[j, t] = az[j, t].astype(jnp.bfloat16)
+                up_copy(j, t).start()
+
+            @pl.when((z > 0) & (z < t))
+            def _():
+                up_copy(j, t).wait_recv()
+                su[j, t] = (az[j, t] + ru[j, t].astype(jnp.float32)).astype(jnp.bfloat16)
+                up_copy(j, t).start()
+        for t in range(nz - 1):
+            @pl.when(z == nz - 1)
+            def _():
+                sd[j, t] = az[j, t].astype(jnp.bfloat16)
+                down_copy(j, t).start()
+
+            @pl.when((z < nz - 1) & (z > t))
+            def _():
+                down_copy(j, t).wait_recv()
+                sd[j, t] = (az[j, t] + rd[j, t].astype(jnp.float32)).astype(jnp.bfloat16)
+                down_copy(j, t).start()
+
+    def stage_final(j):
+        @pl.when(z > 0)
+        def _():
+            up_copy(j, z).wait_recv()
+            az[j, z] = az[j, z] + ru[j, z].astype(jnp.float32)
+
+        @pl.when(z < nz - 1)
+        def _():
+            down_copy(j, z).wait_recv()
+            az[j, z] = az[j, z] + rd[j, z].astype(jnp.float32)
+
+        out_ref[:, j * cols:(j + 1) * cols] = az[j, z].astype(jnp.bfloat16)
+
+    stages = (stage_down, stage_cross, stage_column, stage_chain, stage_final)
+    for wave in range(CHUNKS + len(stages) - 1):
+        for s, stage in enumerate(stages):
+            if 0 <= wave - s < CHUNKS:
+                stage(wave - s)
+
+    for j in range(CHUNKS):
+        for src in range(nz):
+            pl.when((z < nz - 1) & (src <= z))(
+                lambda: block_copy(j, mine + src, UP, src, above).wait_send())
+            pl.when((z > 0) & (src >= z))(
+                lambda: block_copy(j, mine + src, DOWN, src, below).wait_send())
+            block_copy(j, mine + src, CROSS, src, across).wait_send()
+            block_copy(j, mine + src, TWIN, src, twin).wait_send()
+            block_copy(j, other + src, RELAY, src, twin).wait_send()
+        twin_copy(j).wait_send()
+        cross_copy(j).wait_send()
+        for t in range(nz):
+            pl.when(z < t)(lambda: up_copy(j, t).wait_send())
+            pl.when(z > t)(lambda: down_copy(j, t).wait_send())
+
+
+def dense_local(tokens, expert_ids, combine_weights, slot_plan, w_gate, w_up, w_down):
+    nz = lax.axis_size("node")
+    n_dev = nz * lax.axis_size("rank")
+    rows, width = tokens.shape
+    exp_dev, _, ff = w_gate.shape
+    experts = slot_plan.shape[0]
+    cols = width // CHUNKS
+    mix_w = -(-2 * experts // 128) * 128
+    plan = jnp.concatenate(
+        [slot_plan, slot_plan, jnp.full((mix_w - 2 * experts,), -1, jnp.int32)]
+    )[None, :]
+    half = 2 * nz
+    half_rows, col_rows = half * rows, nz * rows
+    bf, f32 = jnp.bfloat16, jnp.float32
+    dma = pltpu.SemaphoreType.DMA
+    vmem = pl.BlockSpec(memory_space=pltpu.VMEM)
+    hbm = pl.BlockSpec(memory_space=pl.ANY)
+    scratch = [
+        pltpu.VMEM((n_dev, rows, cols + (mix_w if j == 0 else 0)), bf) for j in range(CHUNKS)
+    ] + [
+        pltpu.VMEM((2 * exp_dev, width, ff), bf),
+        pltpu.VMEM((exp_dev * ff, width), bf),
+        pltpu.VMEM((2 * exp_dev, n_dev * rows, ff), f32),
+        pltpu.VMEM((n_dev * rows, exp_dev * ff), bf),
+        pltpu.VMEM((CHUNKS, half_rows, cols), bf),
+        pltpu.VMEM((CHUNKS, half_rows, cols), bf),
+        pltpu.VMEM((CHUNKS, half_rows, cols), f32),
+        pltpu.VMEM((CHUNKS, col_rows, cols), bf),
+        pltpu.VMEM((CHUNKS, col_rows, cols), bf),
+        pltpu.VMEM((CHUNKS, nz, rows, cols), f32),
+        pltpu.VMEM((CHUNKS, nz, rows, cols), bf),
+        pltpu.VMEM((CHUNKS, nz, rows, cols), bf),
+        pltpu.VMEM((CHUNKS, nz, rows, cols), bf),
+        pltpu.VMEM((CHUNKS, nz, rows, cols), bf),
+        dma((CHUNKS,)),
+        dma((CHUNKS, 2 * exp_dev)),
+        dma((exp_dev,)),
+        dma((CHUNKS, 5, nz)),
+        dma((CHUNKS, n_dev)),
+        dma((CHUNKS,)),
+        dma((CHUNKS,)),
+        dma((CHUNKS,)),
+        dma((CHUNKS,)),
+        dma((CHUNKS, nz)),
+        dma((CHUNKS, nz)),
+        dma((CHUNKS, nz)),
+        dma((CHUNKS, nz)),
+    ]
+    return pl.pallas_call(
+        functools.partial(kernel, nz, experts),
+        out_shape=jax.ShapeDtypeStruct((rows, width), bf),
+        in_specs=[hbm, vmem, vmem, vmem, hbm, hbm, hbm],
+        out_specs=vmem,
+        scratch_shapes=scratch,
+        compiler_params=pltpu.CompilerParams(
+            collective_id=0, has_side_effects=True, vmem_limit_bytes=60 * 1024 * 1024
+        ),
+    )(tokens, expert_ids, combine_weights, plan, w_gate, w_up, w_down)
+
+
+def local(tokens, expert_ids, combine_weights, slot_plan, w_gate, w_up, w_down):
+    slots = slot_plan.shape[0]
+    rows, top = expert_ids.shape
+    capacity = max(2, (3 * rows * top + 2 * slots - 1) // (2 * slots))
+    fits = 2 * capacity * w_gate.shape[0] >= rows
+    body = dense_local if fits and lax.axis_size("rank") == 2 * CORES else sparse_local
+    return body(tokens, expert_ids, combine_weights, slot_plan, w_gate, w_up, w_down)
+
+
 def solution(mesh):
     in_specs = (
         P(("grp", "node", "rank"), None),

time: 141 us -> 78.2 us (0.55)
  the two profiles are of different devices: /device:TPU:11 before, /device:TPU:0 now
where the time goes in v1:
time: 78.2 us; the launch traced here: 77.8 us
  Pallas kernels  72.1 us (92%)
  local copies, waits for them, and re-layouts  4.32 us (6%)
  other arithmetic  1.38 us (2%)
    pallas_call x1, Pallas kernels, dense_local(): pl.pallas_call(functools.partial(kernel, nz, experts), out_shape=jax.Shap...  72.1 us
    unnamed x3, local copies, waits for them, and re-layouts  4.32 us

profile of v1, /device:TPU:0, one launch (start us, length us, event | category | flops | bytes accessed | tf_op | source)
XLA Modules:
  0.0 77.8 jit_solution(15693430717817277876)
XLA Ops:
  0.0 1.4 %add_bitcast_fusion.plan_ref = s32[1,128]{1,0:T(1,128)} fusion(s32[64]{0:T(128)S(1)} %broadcast_in_dim.6, s32[32]{0:T(128)} %param.10), kind=kLoop, calls=%fused_computation | loop fusion | flops 256 | bytes 896 | tf_op jit(solution)/shard_map/broadcast_in_dim | solution.py:325
  1.4 1.4 %copy.8.ids_ref = s32[32,10]{1,0:T(8,128)} copy(s32[32,10]{0,1:T(8,128)} %param.8) | data formatting | bytes 2560 | tf_op args[1]
  2.8 1.4 %copy.9.wts_ref = s32[32,10]{1,0:T(8,128)} copy(s32[32,10]{0,1:T(8,128)} %param.9) | data formatting | bytes 2560 | tf_op args[2]
  4.1 72.1 %shard_map.73 = bf16[32,2048]{1,0:T(8,128)(2,1)} custom-call(bf16[32,2048]{1,0:T(8,128)(2,1)} %tok_hbm.1, s32[32,10]{1,0:T(8,128)} %copy.8.ids_ref, s32[32,10]{1,0:T(8,128)} %copy.9.wts_ref, s32[1,128]{1,0:T(1,128)} %add_bitcast_fusion.plan_ref, bf16[2,2048,512]{2,1,0:T(8,128)(2,1)} %wg_hbm.1, bf16[2,2048,512]{2,1,0:T(8,128)(2,1)} %wu_hbm.1, ...), custom_call_target="tpu_custom_call" | custom-call | tf_op jit(solution)/shard_map/pallas_call | solution.py:365
  76.2 1.6 %copy.11 = bf16[32,2048]{1,0:T(8,128)(2,1)} copy(bf16[32,2048]{1,0:T(8,128)(2,1)} %shard_map.73) | data formatting | bytes 262144
  (1 shorter events, 0.0 us)

commit v2 on v1

--- a/solution.py
+++ b/solution.py
@@ -9,7 +9,7 @@
 CORES = 2
 CHUNKS = 4
 MESH = pl.DeviceIdType.MESH
-UP, DOWN, CROSS, TWIN, RELAY = range(5)
+CROSS, TWIN, RELAY, COLUMN = range(4)
 
 
 def sparse_local(tokens, expert_ids, combine_weights, slot_plan, w_gate, w_up, w_down):
@@ -52,9 +52,9 @@
     *scratch,
 ):
     bufs = scratch[:CHUNKS]
-    (wgu, wdn, acc, hid, s1, r1, k1, s2, r2, az, su, ru, sd, rd,
+    (wgu, wdn, acc, hid, s1, r1, k1, s2, r2, az, s3, r3,
      own_sem, wgu_sem, wd_sem, send_sem, recv_sem,
-     s1_sem, r1_sem, s2_sem, r2_sem, su_sem, ru_sem, sd_sem, rd_sem) = scratch[CHUNKS:]
+     s1_sem, r1_sem, s2_sem, r2_sem, s3_sem, r3_sem) = scratch[CHUNKS:]
     z = lax.axis_index("node")
     rank = lax.axis_index("rank")
     x, c = rank // CORES, rank % CORES
@@ -66,7 +66,6 @@
     total_rows = 2 * half * rows
     mine = c * half + x * nz
     other = c * half + (1 - x) * nz
-    above, below = {"node": z + 1}, {"node": z - 1}
     across = {"rank": (1 - x) * CORES + c}
     twin = {"rank": x * CORES + (1 - c)}
 
@@ -88,8 +87,8 @@
 
     greet(across)
     greet(twin)
-    pl.when(z < nz - 1)(lambda: greet(above))
-    pl.when(z > 0)(lambda: greet(below))
+    for d in range(1, nz):
+        greet({"node": (z + d) % nz})
 
     gu_copies = []
     for j in range(CHUNKS):
@@ -124,8 +123,7 @@
     parts = jnp.where(low, dense & 255, dense >> 8)
     bufs[0][mine + z, :, cols:] = parts.astype(jnp.float32).astype(jnp.bfloat16)
 
-    peers = 2 + (z < nz - 1).astype(jnp.int32) + (z > 0).astype(jnp.int32)
-    pl.semaphore_wait(barrier, peers)
+    pl.semaphore_wait(barrier, nz + 1)
 
     def block_copy(j, slot, kind, row, device):
         return pltpu.make_async_remote_copy(
@@ -140,38 +138,38 @@
     def arrived(j, slot):
         block_copy(j, slot, RELAY, 0, twin).wait_recv()
 
-    def spread(j, src, go_up, go_down):
-        if go_up:
-            pl.when(z < nz - 1)(lambda: block_copy(j, mine + src, UP, src, above).start())
-        if go_down:
-            pl.when(z > 0)(lambda: block_copy(j, mine + src, DOWN, src, below).start())
+    def spread(j, src):
         block_copy(j, mine + src, CROSS, src, across).start()
         block_copy(j, mine + src, TWIN, src, twin).start()
+
+    def by_distance(dist, step):
+        pl.when(z - dist >= 0)(lambda: step(z - dist))
+        pl.when(z + dist <= nz - 1)(lambda: step(z + dist))
 
     def relay(j, src):
         arrived(j, other + src)
         block_copy(j, other + src, RELAY, src, twin).start()
 
-    def gather_step(j, dist):
-        if dist == 0:
+    def to_column(j, dst):
+        block_copy(j, mine + z, COLUMN + dst, 0, {"node": dst}).start()
+
+    def from_column(j, src):
+        arrived(j, mine + src)
+        spread(j, src)
+
+    def gather_step(j, step):
+        if step == 0:
             own[j].wait()
-            spread(j, z, True, True)
-        elif dist < nz:
-            @pl.when(z - dist >= 0)
-            def _():
-                arrived(j, mine + z - dist)
-                spread(j, z - dist, True, False)
-
-            @pl.when(z + dist <= nz - 1)
-            def _():
-                arrived(j, mine + z + dist)
-                spread(j, z + dist, False, True)
-        if dist >= 1:
-            if dist == 1:
-                relay(j, z)
-            else:
-                pl.when(z - dist + 1 >= 0)(lambda: relay(j, z - dist + 1))
-                pl.when(z + dist - 1 <= nz - 1)(lambda: relay(j, z + dist - 1))
+            for dist in range(nz - 1, 0, -1):
+                by_distance(dist, lambda t: to_column(j, t))
+            spread(j, z)
+        elif step == 1:
+            relay(j, z)
+            for dist in range(1, nz):
+                by_distance(dist, lambda t: from_column(j, t))
+        else:
+            for dist in range(1, nz):
+                by_distance(dist, lambda t: relay(j, t))
 
     def project(j):
         for s in range(half):
@@ -192,13 +190,13 @@
 
         lax.fori_loop(0, 2 * exp_dev, one, 0)
 
-    for wave in range(CHUNKS + nz):
-        for dist in range(nz + 1):
-            j = wave - dist
+    for wave in range(CHUNKS + 2):
+        for step in range(3):
+            j = wave - step
             if 0 <= j < CHUNKS:
-                gather_step(j, dist)
-        if 0 <= wave - nz < CHUNKS:
-            project(wave - nz)
+                gather_step(j, step)
+        if wave >= 2:
+            project(wave - 2)
 
     device = z * lax.axis_size("rank") + rank
     mixes = bufs[0][:, :, cols:].reshape(total_rows, mix_w).astype(jnp.float32)
@@ -227,11 +225,8 @@
     def cross_copy(j):
         return push(s2.at[j], r2.at[j], s2_sem.at[j], r2_sem.at[j], across)
 
-    def up_copy(j, t):
-        return push(su.at[j, t], ru.at[j, t], su_sem.at[j, t], ru_sem.at[j, t], above)
-
-    def down_copy(j, t):
-        return push(sd.at[j, t], rd.at[j, t], sd_sem.at[j, t], rd_sem.at[j, t], below)
+    def column_copy(j, dst, src):
+        return push(s3.at[j, dst], r3.at[j, src], s3_sem.at[j, dst], r3_sem.at[j, src], {"node": dst})
 
     def stage_down(j):
         w = wdn[:, j * cols:(j + 1) * cols]
@@ -253,46 +248,21 @@
         cross_copy(j).wait_recv()
         near = pl.ds(x * col_rows, col_rows)
         total = k1[j, near, :] + r1[j, near, :].astype(jnp.float32) + r2[j].astype(jnp.float32)
-        az[j] = total.reshape(nz, rows, cols)
-
-    def stage_chain(j):
-        for t in range(nz - 1, 0, -1):
-            @pl.when(z == 0)
-            def _():
-                su[j, t] = az[j, t].astype(jnp.bfloat16)
-                up_copy(j, t).start()
-
-            @pl.when((z > 0) & (z < t))
-            def _():
-                up_copy(j, t).wait_recv()
-                su[j, t] = (az[j, t] + ru[j, t].astype(jnp.float32)).astype(jnp.bfloat16)
-                up_copy(j, t).start()
-        for t in range(nz - 1):
-            @pl.when(z == nz - 1)
-            def _():
-                sd[j, t] = az[j, t].astype(jnp.bfloat16)
-                down_copy(j, t).start()
-
-            @pl.when((z < nz - 1) & (z > t))
-            def _():
-                down_copy(j, t).wait_recv()
-                sd[j, t] = (az[j, t] + rd[j, t].astype(jnp.float32)).astype(jnp.bfloat16)
-                down_copy(j, t).start()
+        total = total.reshape(nz, rows, cols)
+        az[j] = total
+        s3[j] = total.astype(jnp.bfloat16)
+        for dist in range(nz - 1, 0, -1):
+            by_distance(dist, lambda t: column_copy(j, t, z).start())
 
     def stage_final(j):
-        @pl.when(z > 0)
-        def _():
-            up_copy(j, z).wait_recv()
-            az[j, z] = az[j, z] + ru[j, z].astype(jnp.float32)
-
-        @pl.when(z < nz - 1)
-        def _():
-            down_copy(j, z).wait_recv()
-            az[j, z] = az[j, z] + rd[j, z].astype(jnp.float32)
-
-        out_ref[:, j * cols:(j + 1) * cols] = az[j, z].astype(jnp.bfloat16)
-
-    stages = (stage_down, stage_cross, stage_column, stage_chain, stage_final)
+        total = az[j, z]
+        for d in range(1, nz):
+            t = (z + d) % nz
+            column_copy(j, z, t).wait_recv()
+            total += r3[j, t].astype(jnp.float32)
+        out_ref[:, j * cols:(j + 1) * cols] = total.astype(jnp.bfloat16)
+
+    stages = (stage_down, stage_cross, stage_column, stage_final)
     for wave in range(CHUNKS + len(stages) - 1):
         for s, stage in enumerate(stages):
             if 0 <= wave - s < CHUNKS:
@@ -300,18 +270,15 @@
 
     for j in range(CHUNKS):
         for src in range(nz):
-            pl.when((z < nz - 1) & (src <= z))(
-                lambda: block_copy(j, mine + src, UP, src, above).wait_send())
-            pl.when((z > 0) & (src >= z))(
-                lambda: block_copy(j, mine + src, DOWN, src, below).wait_send())
             block_copy(j, mine + src, CROSS, src, across).wait_send()
             block_copy(j, mine + src, TWIN, src, twin).wait_send()
             block_copy(j, other + src, RELAY, src, twin).wait_send()
         twin_copy(j).wait_send()
         cross_copy(j).wait_send()
-        for t in range(nz):
-            pl.when(z < t)(lambda: up_copy(j, t).wait_send())
-            pl.when(z > t)(lambda: down_copy(j, t).wait_send())
+        for d in range(1, nz):
+            t = (z + d) % nz
+            block_copy(j, mine + z, COLUMN + t, 0, {"node": t}).wait_send()
+            column_copy(j, t, z).wait_send()
 
 
 def dense_local(tokens, expert_ids, combine_weights, slot_plan, w_gate, w_up, w_down):
@@ -346,19 +313,15 @@
         pltpu.VMEM((CHUNKS, nz, rows, cols), f32),
         pltpu.VMEM((CHUNKS, nz, rows, cols), bf),
         pltpu.VMEM((CHUNKS, nz, rows, cols), bf),
-        pltpu.VMEM((CHUNKS, nz, rows, cols), bf),
-        pltpu.VMEM((CHUNKS, nz, rows, cols), bf),
         dma((CHUNKS,)),
         dma((CHUNKS, 2 * exp_dev)),
         dma((exp_dev,)),
-        dma((CHUNKS, 5, nz)),
+        dma((CHUNKS, 3 + nz, nz)),
         dma((CHUNKS, n_dev)),
         dma((CHUNKS,)),
         dma((CHUNKS,)),
         dma((CHUNKS,)),
         dma((CHUNKS,)),
-        dma((CHUNKS, nz)),
-        dma((CHUNKS, nz)),
         dma((CHUNKS, nz)),
         dma((CHUNKS, nz)),
     ]

time: 78.2 us -> 59.6 us (0.76)
  Pallas kernels: 72.1 us -> 53.5 us
    pallas_call x1, Pallas kernels: 72.1 us -> 53.5 us  [dense_local(): pl.pallas_call(functools.partial(kernel, nz, experts), out_shape=jax.Shap...]
where the time goes in v2:
time: 59.6 us; the launch traced here: 59.2 us
  Pallas kernels  53.5 us (90%)
  local copies, waits for them, and re-layouts  4.32 us (7%)
  other arithmetic  1.38 us (2%)
    pallas_call x1, Pallas kernels, dense_local(): pl.pallas_call(functools.partial(kernel, nz, experts), out_shape=jax.Shap...  53.5 us
    unnamed x3, local copies, waits for them, and re-layouts  4.32 us
    broadcast_in_dim x1, other arithmetic, dense_local(): jnp.concatenate([slot_plan, slot_plan, jnp.full((mix_w - 2 * experts,), -...  1.38 us

profile of v2, /device:TPU:0, one launch (start us, length us, event | category | flops | bytes accessed | tf_op | source)
XLA Modules:
  0.0 59.2 jit_solution(15950708837106710437)
XLA Ops:
  0.0 1.4 %add_bitcast_fusion.plan_ref = s32[1,128]{1,0:T(1,128)} fusion(s32[64]{0:T(128)S(1)} %broadcast_in_dim.6, s32[32]{0:T(128)} %param.10), kind=kLoop, calls=%fused_computation | loop fusion | flops 256 | bytes 896 | tf_op jit(solution)/shard_map/broadcast_in_dim | solution.py:292
  1.4 1.4 %copy.8.ids_ref = s32[32,10]{1,0:T(8,128)} copy(s32[32,10]{0,1:T(8,128)} %param.8) | data formatting | bytes 2560 | tf_op args[1]
  2.8 1.4 %copy.9.wts_ref = s32[32,10]{1,0:T(8,128)} copy(s32[32,10]{0,1:T(8,128)} %param.9) | data formatting | bytes 2560 | tf_op args[2]
  4.1 53.5 %shard_map.73 = bf16[32,2048]{1,0:T(8,128)(2,1)} custom-call(bf16[32,2048]{1,0:T(8,128)(2,1)} %tok_hbm.1, s32[32,10]{1,0:T(8,128)} %copy.8.ids_ref, s32[32,10]{1,0:T(8,128)} %copy.9.wts_ref, s32[1,128]{1,0:T(1,128)} %add_bitcast_fusion.plan_ref, bf16[2,2048,512]{2,1,0:T(8,128)(2,1)} %wg_hbm.1, bf16[2,2048,512]{2,1,0:T(8,128)(2,1)} %wu_hbm.1, ...), custom_call_target="tpu_custom_call" | custom-call | tf_op jit(solution)/shard_map/pallas_call | solution.py:328
  57.6 1.6 %copy.11 = bf16[32,2048]{1,0:T(8,128)(2,1)} copy(bf16[32,2048]{1,0:T(8,128)(2,1)} %shard_map.73) | data formatting | bytes 262144
  (1 shorter events, 0.0 us)

commit v3 on v2

--- a/solution.py
+++ b/solution.py
@@ -8,6 +8,8 @@
 
 CORES = 2
 CHUNKS = 4
+PIECES = 4
+LAGS = (0, 1, 3, 5)
 MESH = pl.DeviceIdType.MESH
 CROSS, TWIN, RELAY, COLUMN = range(4)
 
@@ -113,15 +115,22 @@
         copy.start()
 
     mix_w = bufs[0].shape[2] - cols
-    lane = lax.broadcasted_iota(jnp.int32, (rows, mix_w), 1)
-    low = lane >= experts
-    expert = jnp.where(low, lane - experts, lane)
+    line = lax.broadcasted_iota(jnp.int32, (mix_w, rows), 0)
+    low = line >= experts
+    expert = jnp.where(low, line - experts, line)
     ids, wts = ids_ref[...], wts_ref[...]
-    dense = jnp.zeros((rows, mix_w), jnp.int32)
-    for k in range(ids.shape[1]):
-        dense += jnp.where(ids[:, k:k + 1] == expert, wts[:, k:k + 1], 0)
-    parts = jnp.where(low, dense & 255, dense >> 8)
-    bufs[0][mine + z, :, cols:] = parts.astype(jnp.float32).astype(jnp.bfloat16)
+    dense = jnp.zeros((mix_w, rows), jnp.int32)
+    for k in range(ids.shape[0]):
+        dense += jnp.where(ids[k:k + 1, :] == expert, wts[k:k + 1, :], 0)
+    parts = jnp.where(low, dense & 255, dense >> 8).astype(jnp.float32).astype(jnp.bfloat16)
+    eye = (
+        lax.broadcasted_iota(jnp.int32, (rows, rows), 0)
+        == lax.broadcasted_iota(jnp.int32, (rows, rows), 1)
+    ).astype(jnp.float32).astype(jnp.bfloat16)
+    turned = lax.dot_general(
+        eye, parts, (((1,), (1,)), ((), ())), preferred_element_type=jnp.float32
+    )
+    bufs[0][mine + z, :, cols:] = turned.astype(jnp.bfloat16)
 
     pl.semaphore_wait(barrier, nz + 1)
 
@@ -157,54 +166,58 @@
         arrived(j, mine + src)
         spread(j, src)
 
-    def gather_step(j, step):
-        if step == 0:
-            own[j].wait()
-            for dist in range(nz - 1, 0, -1):
-                by_distance(dist, lambda t: to_column(j, t))
-            spread(j, z)
-        elif step == 1:
-            relay(j, z)
-            for dist in range(1, nz):
-                by_distance(dist, lambda t: from_column(j, t))
-        else:
-            for dist in range(1, nz):
-                by_distance(dist, lambda t: relay(j, t))
-
-    def project(j):
+    def pieces_of(j):
+        steps = [lambda: relay(j, z)]
+        for dist in range(1, nz):
+            steps.append(lambda dist=dist: by_distance(dist, lambda t: from_column(j, t)))
+        return steps
+
+    def relays_of(j):
+        return [
+            lambda dist=dist: by_distance(dist, lambda t: relay(j, t)) for dist in range(1, nz)
+        ]
+
+    def dot_piece(j, i):
+        block = bufs[j][:, :, :cols].reshape(total_rows, cols)
+        part = jnp.dot(
+            block, wgu[i, pl.ds(j * cols, cols), :], preferred_element_type=jnp.float32
+        )
+        acc[i] = part if j == 0 else acc[i] + part
+
+    def ready(j):
         for s in range(half):
             arrived(j, (1 - c) * half + s)
         for copy in gu_copies[j]:
             copy.wait()
 
-        def one(i, carry):
-            block = bufs[j][:, :, :cols].reshape(total_rows, cols)
-            part = jnp.dot(
-                block, wgu[i, pl.ds(j * cols, cols), :], preferred_element_type=jnp.float32
-            )
-            if j == 0:
-                acc[i] = part
-            else:
-                acc[i] = acc[i] + part
-            return carry
-
-        lax.fori_loop(0, 2 * exp_dev, one, 0)
-
+    for j in range(CHUNKS):
+        own[j].wait()
+        for dist in range(nz - 1, 0, -1):
+            by_distance(dist, lambda t: to_column(j, t))
+        spread(j, z)
     for wave in range(CHUNKS + 2):
-        for step in range(3):
-            j = wave - step
-            if 0 <= j < CHUNKS:
-                gather_step(j, step)
+        moves = []
+        if wave < CHUNKS:
+            moves += pieces_of(wave)
+        if 1 <= wave <= CHUNKS:
+            moves += relays_of(wave - 1)
+        dots = []
         if wave >= 2:
-            project(wave - 2)
+            ready(wave - 2)
+            dots = [lambda i=i: dot_piece(wave - 2, i) for i in range(2 * exp_dev)]
+        for i in range(max(len(moves), len(dots))):
+            if i < len(dots):
+                dots[i]()
+            if i < len(moves):
+                moves[i]()
 
     device = z * lax.axis_size("rank") + rank
     mixes = bufs[0][:, :, cols:].reshape(total_rows, mix_w).astype(jnp.float32)
-    lane_row = lax.broadcasted_iota(jnp.int32, (1, mix_w), 1)
-    unit = jnp.where(lane_row < experts, 256.0 / 65536.0, 1.0 / 65536.0)
+    high, small = mixes[:, :experts], mixes[:, experts:2 * experts]
+    counts = high * (256.0 / 65536.0) + small * (1.0 / 65536.0)
     for e in range(exp_dev):
-        pick = jnp.where(plan_ref[...] == device * exp_dev + e, unit, 0.0)
-        scale = jnp.sum(mixes * pick, axis=1, keepdims=True)
+        pick = jnp.where(plan_ref[...] == device * exp_dev + e, 1.0, 0.0)
+        scale = jnp.sum(counts * pick, axis=1, keepdims=True)
         gate = acc[2 * e]
         value = gate / (1.0 + jnp.exp(-gate)) * acc[2 * e + 1]
         hid[:, e * ff:(e + 1) * ff] = (value * scale).astype(jnp.bfloat16)
@@ -212,6 +225,7 @@
         copy.wait()
 
     half_rows = half * rows
+    span = width // PIECES
 
     def push(src, dst, ssem, rsem, dev):
         return pltpu.make_async_remote_copy(
@@ -229,7 +243,7 @@
         return push(s3.at[j, dst], r3.at[j, src], s3_sem.at[j, dst], r3_sem.at[j, src], {"node": dst})
 
     def stage_down(j):
-        w = wdn[:, j * cols:(j + 1) * cols]
+        w = wdn[:, j * span:(j + 1) * span]
         s1[j] = jnp.dot(
             hid[pl.ds((1 - c) * half_rows, half_rows), :], w, preferred_element_type=jnp.float32
         ).astype(jnp.bfloat16)
@@ -248,7 +262,7 @@
         cross_copy(j).wait_recv()
         near = pl.ds(x * col_rows, col_rows)
         total = k1[j, near, :] + r1[j, near, :].astype(jnp.float32) + r2[j].astype(jnp.float32)
-        total = total.reshape(nz, rows, cols)
+        total = total.reshape(nz, rows, span)
         az[j] = total
         s3[j] = total.astype(jnp.bfloat16)
         for dist in range(nz - 1, 0, -1):
@@ -260,25 +274,27 @@
             t = (z + d) % nz
             column_copy(j, z, t).wait_recv()
             total += r3[j, t].astype(jnp.float32)
-        out_ref[:, j * cols:(j + 1) * cols] = total.astype(jnp.bfloat16)
+        out_ref[:, j * span:(j + 1) * span] = total.astype(jnp.bfloat16)
 
     stages = (stage_down, stage_cross, stage_column, stage_final)
-    for wave in range(CHUNKS + len(stages) - 1):
-        for s, stage in enumerate(stages):
-            if 0 <= wave - s < CHUNKS:
-                stage(wave - s)
+    for wave in range(PIECES + LAGS[-1]):
+        for lag, stage in zip(LAGS, stages):
+            if 0 <= wave - lag < PIECES:
+                stage(wave - lag)
 
     for j in range(CHUNKS):
         for src in range(nz):
             block_copy(j, mine + src, CROSS, src, across).wait_send()
             block_copy(j, mine + src, TWIN, src, twin).wait_send()
             block_copy(j, other + src, RELAY, src, twin).wait_send()
+        for d in range(1, nz):
+            t = (z + d) % nz
+            block_copy(j, mine + z, COLUMN + t, 0, {"node": t}).wait_send()
+    for j in range(PIECES):
         twin_copy(j).wait_send()
         cross_copy(j).wait_send()
         for d in range(1, nz):
-            t = (z + d) % nz
-            block_copy(j, mine + z, COLUMN + t, 0, {"node": t}).wait_send()
-            column_copy(j, t, z).wait_send()
+            column_copy(j, (z + d) % nz, z).wait_send()
 
 
 def dense_local(tokens, expert_ids, combine_weights, slot_plan, w_gate, w_up, w_down):
@@ -287,11 +303,8 @@
     rows, width = tokens.shape
     exp_dev, _, ff = w_gate.shape
     experts = slot_plan.shape[0]
-    cols = width // CHUNKS
+    cols, span = width // CHUNKS, width // PIECES
     mix_w = -(-2 * experts // 128) * 128
-    plan = jnp.concatenate(
-        [slot_plan, slot_plan, jnp.full((mix_w - 2 * experts,), -1, jnp.int32)]
-    )[None, :]
     half = 2 * nz
     half_rows, col_rows = half * rows, nz * rows
     bf, f32 = jnp.bfloat16, jnp.float32
@@ -305,25 +318,25 @@
         pltpu.VMEM((exp_dev * ff, width), bf),
         pltpu.VMEM((2 * exp_dev, n_dev * rows, ff), f32),
         pltpu.VMEM((n_dev * rows, exp_dev * ff), bf),
-        pltpu.VMEM((CHUNKS, half_rows, cols), bf),
-        pltpu.VMEM((CHUNKS, half_rows, cols), bf),
-        pltpu.VMEM((CHUNKS, half_rows, cols), f32),
-        pltpu.VMEM((CHUNKS, col_rows, cols), bf),
-        pltpu.VMEM((CHUNKS, col_rows, cols), bf),
-        pltpu.VMEM((CHUNKS, nz, rows, cols), f32),
-        pltpu.VMEM((CHUNKS, nz, rows, cols), bf),
-        pltpu.VMEM((CHUNKS, nz, rows, cols), bf),
+        pltpu.VMEM((PIECES, half_rows, span), bf),
+        pltpu.VMEM((PIECES, half_rows, span), bf),
+        pltpu.VMEM((PIECES, half_rows, span), f32),
+        pltpu.VMEM((PIECES, col_rows, span), bf),
+        pltpu.VMEM((PIECES, col_rows, span), bf),
+        pltpu.VMEM((PIECES, nz, rows, span), f32),
+        pltpu.VMEM((PIECES, nz, rows, span), bf),
+        pltpu.VMEM((PIECES, nz, rows, span), bf),
         dma((CHUNKS,)),
         dma((CHUNKS, 2 * exp_dev)),
         dma((exp_dev,)),
         dma((CHUNKS, 3 + nz, nz)),
         dma((CHUNKS, n_dev)),
-        dma((CHUNKS,)),
-        dma((CHUNKS,)),
-        dma((CHUNKS,)),
-        dma((CHUNKS,)),
-        dma((CHUNKS, nz)),
-        dma((CHUNKS, nz)),
+        dma((PIECES,)),
+        dma((PIECES,)),
+        dma((PIECES,)),
+        dma((PIECES,)),
+        dma((PIECES, nz)),
+        dma((PIECES, nz)),
     ]
     return pl.pallas_call(
         functools.partial(kernel, nz, experts),
@@ -334,7 +347,7 @@
         compiler_params=pltpu.CompilerParams(
             collective_id=0, has_side_effects=True, vmem_limit_bytes=60 * 1024 * 1024
         ),
-    )(tokens, expert_ids, combine_weights, plan, w_gate, w_up, w_down)
+    )(tokens, expert_ids.T, combine_weights.T, slot_plan[None, :], w_gate, w_up, w_down)
 
 
 def local(tokens, expert_ids, combine_weights, slot_plan, w_gate, w_up, w_down):

time: 59.6 us -> 52.6 us (0.88)
  local copies, waits for them, and re-layouts: 4.32 us -> 1.57 us
  Pallas kernels: 53.5 us -> 50.8 us
  other arithmetic: 1.38 us -> 0 us
    unnamed x3 -> x1, local copies, waits for them, and re-layouts: 4.32 us -> 1.57 us
    pallas_call x1, Pallas kernels: 53.5 us -> 50.8 us  [dense_local(): pl.pallas_call(functools.partial(kernel, nz, experts), out_shape=jax.Shap...]
    broadcast_in_dim x1 -> x0, other arithmetic: 1.38 us -> none  [dense_local(): jnp.concatenate([slot_plan, slot_plan, jnp.full((mix_w - 2 * experts,), -...]
where the time goes in v3:
time: 52.6 us; the launch traced here: 52.4 us
  Pallas kernels  50.8 us (97%)
  local copies, waits for them, and re-layouts  1.57 us (3%)
    pallas_call x1, Pallas kernels, dense_local(): pl.pallas_call(functools.partial(kernel, nz, experts), out_shape=jax.Shap...  50.8 us
    unnamed x1, local copies, waits for them, and re-layouts  1.57 us

profile of v3, /device:TPU:0, one launch (start us, length us, event | category | flops | bytes accessed | tf_op | source)
XLA Modules:
  0.0 52.4 jit_solution(5231246285126579927)
XLA Ops:
  0.0 50.8 %shard_map.73 = bf16[32,2048]{1,0:T(8,128)(2,1)} custom-call(bf16[32,2048]{1,0:T(8,128)(2,1)} %tok_hbm.1, s32[10,32]{1,0:T(8,128)} %bitcast.3, s32[10,32]{1,0:T(8,128)} %bitcast.4, s32[1,32]{1,0:T(1,128)} %bitcast.5, bf16[2,2048,512]{2,1,0:T(8,128)(2,1)} %wg_hbm.1, bf16[2,2048,512]{2,1,0:T(8,128)(2,1)} %wu_hbm.1, bf16[2,512,2048]{2,1,0:T(8,128)(2,1)} %wd_hbm.1), custom_call_target="tpu_custom_call" | custom-call | tf_op jit(solution)/shard_map/pallas_call | solution.py:341
  50.8 1.6 %copy.9 = bf16[32,2048]{1,0:T(8,128)(2,1)} copy(bf16[32,2048]{1,0:T(8,128)(2,1)} %shard_map.73) | data formatting | bytes 262144

commit v4 on v3

--- a/solution.py
+++ b/solution.py
@@ -7,7 +7,7 @@
 from jax.sharding import PartitionSpec as P
 
 CORES = 2
-CHUNKS = 4
+CHUNKS = 2
 PIECES = 4
 LAGS = (0, 1, 3, 5)
 MESH = pl.DeviceIdType.MESH
@@ -159,23 +159,27 @@
         arrived(j, other + src)
         block_copy(j, other + src, RELAY, src, twin).start()
 
-    def to_column(j, dst):
-        block_copy(j, mine + z, COLUMN + dst, 0, {"node": dst}).start()
-
-    def from_column(j, src):
-        arrived(j, mine + src)
-        spread(j, src)
-
-    def pieces_of(j):
-        steps = [lambda: relay(j, z)]
-        for dist in range(1, nz):
-            steps.append(lambda dist=dist: by_distance(dist, lambda t: from_column(j, t)))
-        return steps
-
-    def relays_of(j):
-        return [
-            lambda dist=dist: by_distance(dist, lambda t: relay(j, t)) for dist in range(1, nz)
-        ]
+    def upward(j, src):
+        return block_copy(j, mine + src, COLUMN, src, {"node": z + 1})
+
+    def downward(j, src):
+        return block_copy(j, mine + src, COLUMN + 1, src, {"node": z - 1})
+
+    def from_column(j, dist):
+        @pl.when(z - dist >= 0)
+        def _():
+            arrived(j, mine + z - dist)
+            pl.when(z < nz - 1)(lambda: upward(j, z - dist).start())
+            spread(j, z - dist)
+
+        @pl.when(z + dist <= nz - 1)
+        def _():
+            arrived(j, mine + z + dist)
+            pl.when(z > 0)(lambda: downward(j, z + dist).start())
+            spread(j, z + dist)
+
+    def relays_of(j, dist):
+        return [lambda: by_distance(dist, lambda t: relay(j, t))] if dist else [lambda: relay(j, z)]
 
     def dot_piece(j, i):
         block = bufs[j][:, :, :cols].reshape(total_rows, cols)
@@ -192,19 +196,23 @@
 
     for j in range(CHUNKS):
         own[j].wait()
-        for dist in range(nz - 1, 0, -1):
-            by_distance(dist, lambda t: to_column(j, t))
+        pl.when(z < nz - 1)(lambda: upward(j, z).start())
+        pl.when(z > 0)(lambda: downward(j, z).start())
         spread(j, z)
-    for wave in range(CHUNKS + 2):
+    for wave in range(CHUNKS + nz):
         moves = []
-        if wave < CHUNKS:
-            moves += pieces_of(wave)
-        if 1 <= wave <= CHUNKS:
-            moves += relays_of(wave - 1)
+        for dist in range(1, nz):
+            j = wave - dist + 1
+            if 0 <= j < CHUNKS:
+                moves.append(lambda j=j, dist=dist: from_column(j, dist))
+        for dist in range(nz):
+            j = wave - dist
+            if 0 <= j < CHUNKS:
+                moves += relays_of(j, dist)
         dots = []
-        if wave >= 2:
-            ready(wave - 2)
-            dots = [lambda i=i: dot_piece(wave - 2, i) for i in range(2 * exp_dev)]
+        if wave >= nz:
+            ready(wave - nz)
+            dots = [lambda i=i: dot_piece(wave - nz, i) for i in range(2 * exp_dev)]
         for i in range(max(len(moves), len(dots))):
             if i < len(dots):
                 dots[i]()
@@ -287,9 +295,9 @@
             block_copy(j, mine + src, CROSS, src, across).wait_send()
             block_copy(j, mine + src, TWIN, src, twin).wait_send()
             block_copy(j, other + src, RELAY, src, twin).wait_send()
-        for d in range(1, nz):
-            t = (z + d) % nz
-            block_copy(j, mine + z, COLUMN + t, 0, {"node": t}).wait_send()
+        for src in range(nz):
+            pl.when((z < nz - 1) & (src <= z))(lambda: upward(j, src).wait_send())
+            pl.when((z > 0) & (src >= z))(lambda: downward(j, src).wait_send())
     for j in range(PIECES):
         twin_copy(j).wait_send()
         cross_copy(j).wait_send()

time: 52.6 us -> 48.9 us (0.930)
  Pallas kernels: 50.8 us -> 47.1 us
    pallas_call x1, Pallas kernels: 50.8 us -> 47.1 us  [dense_local(): pl.pallas_call(functools.partial(kernel, nz, experts), out_shape=jax.Shap...]
where the time goes in v4:
time: 48.9 us; the launch traced here: 48.7 us
  Pallas kernels  47.1 us (96%)
  local copies, waits for them, and re-layouts  1.57 us (3%)
    pallas_call x1, Pallas kernels, dense_local(): pl.pallas_call(functools.partial(kernel, nz, experts), out_shape=jax.Shap...  47.1 us
    unnamed x1, local copies, waits for them, and re-layouts  1.57 us

profile of v4, /device:TPU:0, one launch (start us, length us, event | category | flops | bytes accessed | tf_op | source)
XLA Modules:
  0.0 48.7 jit_solution(11046809326920433492)
XLA Ops:
  0.0 47.1 %shard_map.73 = bf16[32,2048]{1,0:T(8,128)(2,1)} custom-call(bf16[32,2048]{1,0:T(8,128)(2,1)} %tok_hbm.1, s32[10,32]{1,0:T(8,128)} %bitcast.3, s32[10,32]{1,0:T(8,128)} %bitcast.4, s32[1,32]{1,0:T(1,128)} %bitcast.5, bf16[2,2048,512]{2,1,0:T(8,128)(2,1)} %wg_hbm.1, bf16[2,2048,512]{2,1,0:T(8,128)(2,1)} %wu_hbm.1, bf16[2,512,2048]{2,1,0:T(8,128)(2,1)} %wd_hbm.1), custom_call_target="tpu_custom_call" | custom-call | tf_op jit(solution)/shard_map/pallas_call | solution.py:349
  47.1 1.6 %copy.9 = bf16[32,2048]{1,0:T(8,128)(2,1)} copy(bf16[32,2048]{1,0:T(8,128)(2,1)} %shard_map.73) | data formatting | bytes 262144
